TPU v7x, 128 devices: a whole 4x4x4 slice. The times are simulated.
128 devices in a mesh: sample: 4 (over z), marker: 32 (over y, x, core).
Axes of the slice: x: 4, y: 4, z: 4, core: 2. Of those that a mesh axis runs over, the one named last changes fastest.
Arguments:
- genotypes: bfloat16 [8192, 131072], P('sample', 'marker'), may hold values from -6 to 6
- phenotypes: float32 [16, 8192], P(None, 'sample'), may hold values from -6 to 6
- message: float32 [16, 131072], P(None, 'marker'), may hold values from -6 to 6
- probes: float32 [112, 131072], P(None, 'marker'), may hold values from -16 to 16
- inclusion: float32 [16], replicated, may hold values from 0.3 to 0.6
- slab_ratio: float32 [16], replicated, may hold values from 0.25 to 0.67
- input_precision: float32 [16], replicated, may hold values from 0.5 to 2
- noise_precision: float32 [16], replicated, may hold values from 4 to 16
Outputs:
- estimate: float32 [16, 131072], P(None, 'marker')
- lmmse_estimate: float32 [16, 131072], P(None, 'marker')
All inputs are finite; a program needn't handle non-finite values.
Results may differ from a plain program's by a relative error of at most 0.0013.
Values may be sent and summed in bfloat16 or wider, within the bound.
A program may use at most 128 MiB of HBM per device.

v0:
```python
import jax
import jax.numpy as jnp
from jax import lax
from jax.sharding import PartitionSpec as P

MARKERS = 131072
ITERS = 2


def denoise(signal, precision, shrink, logit_base):
    energy = shrink * precision * signal * signal
    weight = jax.nn.sigmoid(logit_base + 0.5 * energy)
    return (shrink * weight * signal, shrink * weight * (1.0 + (1.0 - weight) * energy))


def contract_rows(vectors, genotypes):
    return lax.dot_general(
        vectors, genotypes, (((1,), (1,)), ((), ())), preferred_element_type=jnp.float32
    )


def project(vectors_b, genotypes, offset):
    partial_value = contract_rows(vectors_b, genotypes)
    predicted = lax.psum(partial_value, "marker")
    if offset is not None:
        predicted = offset - predicted
    predicted_b = predicted.astype(jnp.bfloat16)
    widened = predicted_b.astype(jnp.float32)
    back_sum = jnp.dot(predicted_b, genotypes, preferred_element_type=jnp.float32)
    return (back_sum, jnp.sum(widened * widened, axis=1))


def per_device(
    genotypes, phenotypes, message, probes, inclusion, slab_ratio, input_precision, noise_precision
):
    people = genotypes.shape[0] * lax.axis_size("sample")
    traits = message.shape[0]
    copies = probes.shape[0] // traits + 1
    shrink = (slab_ratio / (1.0 + slab_ratio))[:, None]
    odds = jnp.log(inclusion / (1.0 - inclusion))[:, None]
    logit_base = odds + 0.5 * jnp.log(1.0 - shrink)
    first, slopes = denoise(message, input_precision[:, None], shrink, logit_base)
    first_slope = lax.psum(jnp.sum(slopes, axis=1), "marker") / MARKERS
    second_precision = input_precision * (1.0 - first_slope) / first_slope
    centre = (first - first_slope[:, None] * message) / (1.0 - first_slope)[:, None]
    start_back, unused_square = project(centre.astype(jnp.bfloat16), genotypes, phenotypes)
    start_back = lax.psum(start_back, "sample")
    start_res = noise_precision[:, None] / people * start_back
    scale_col = jnp.tile(noise_precision / people, copies)[:, None]
    prec_col = jnp.tile(second_precision, copies)[:, None]
    iterate = jnp.concatenate([centre, jnp.zeros(probes.shape, jnp.float32)], axis=0)
    residual = jnp.concatenate([start_res, probes], axis=0)
    direction = residual
    norm_start = lax.psum(jnp.sum(residual * residual, axis=1), "marker")
    norm_now = norm_start
    for iteration in range(ITERS):
        back_sum, square = project(direction.astype(jnp.bfloat16), genotypes, None)
        back_sum = lax.psum(back_sum, "sample")
        applied = scale_col * back_sum + prec_col * direction
        curvature = lax.psum(jnp.sum(direction * applied, axis=1), "marker")
        step_size = norm_now / curvature
        iterate = iterate + step_size[:, None] * direction
        if iteration + 1 < ITERS:
            residual = residual - step_size[:, None] * applied
            norm_next = lax.psum(jnp.sum(residual * residual, axis=1), "marker")
            beta_ratio = norm_next / norm_now
            direction = residual + beta_ratio[:, None] * direction
            norm_now = norm_next
    lmmse_estimate = iterate[:traits]
    probe_local = jnp.sum(
        jnp.sum(probes * iterate[traits:], axis=1).reshape(copies - 1, traits), axis=0
    )
    probe_dot = lax.psum(probe_local, "marker")
    probe_norm = jnp.sum(norm_start[traits:].reshape(copies - 1, traits), axis=0)
    second_slope = second_precision * probe_dot / (probe_norm + 1e-06)
    next_precision = second_precision * (1.0 - second_slope) / second_slope
    next_message = (lmmse_estimate - second_slope[:, None] * centre) / (1.0 - second_slope)[:, None]
    slab_var = slab_ratio / input_precision
    next_shrink = (slab_var * next_precision / (1.0 + slab_var * next_precision))[:, None]
    next_base = odds + 0.5 * jnp.log(1.0 - next_shrink)
    estimate, unused_slopes = denoise(next_message, next_precision[:, None], next_shrink, next_base)
    return (estimate, lmmse_estimate)


def solution(mesh):
    return jax.shard_map(
        per_device,
        mesh=mesh,
        in_specs=(
            P("sample", "marker"),
            P(None, "sample"),
            P(None, "marker"),
            P(None, "marker"),
            P(),
            P(),
            P(),
            P(),
        ),
        out_specs=(P(None, "marker"), P(None, "marker")),
        check_vma=False,
    )
```

profile of v0, /device:TPU:1, one launch (start us, length us, event | category | flops | bytes accessed | tf_op | source)
XLA Modules:
  0.0 946.0 jit_solution(1127837189394486947)
XLA Ops:
  7.2 0.0 all-reduce.9.cloned.1.call-start
  7.2 0.7 multiply_add_fusion.4
  7.9 0.7 mul.192
  8.6 1.3 multiply_reduce_fusion.4
  9.8 63.8 %psum.84 = f32[16]{0:T(128)S(1)} all-reduce(f32[16]{0:T(128)S(1)} %multiply_reduce_fusion.4), channel_id=1, replica_groups=mesh['sample'=4,'marker'=32] {'marker'}, use_global_device_ids=true, to_apply=%region_1.0 | all-reduce | flops 16 | bytes 128 | tf_op jit(solution)/shard_map/psum | solution.py:43
  73.6 0.7 multiply_divide_fusion.1
  74.3 1.1 subtract_divide_fusion
  75.4 0.0 copy-start.3
  75.4 10.9 %fusion.17 = f32[16,2048]{1,0:T(8,128)} fusion(bf16[2048,4096]{1,0:T(8,128)(2,1)} %param.8, f32[16,4096]{1,0:T(8,128)S(1)} %subtract_divide_fusion), kind=kOutput, calls=%fused_computation.33 | convolution fusion | flops 268500992 | bytes 17170432 | tf_op jit(solution)/shard_map/dot_general | solution.py:17
  86.3 0.0 all-reduce.9.cloned.1.call-update
  86.3 0.0 copy-start.6
  86.3 0.0 copy-start
  86.4 0.0 all-reduce.11.cloned.1.call-start
  86.4 102.7 %all-reduce.9.cloned.1.call-done = f32[16,2048]{1,0:T(8,128)} async-done(((f32[16,2048]{1,0:T(8,128)}), f32[16,2048]{1,0:T(8,128)}) %all-reduce.9.cloned.1.call-update) | async-done | bytes 131088 | tf_op jit(solution)/shard_map/psum | solution.py:24
  189.1 0.0 copy-done.3
  189.1 8.8 fusion.19
  197.9 0.0 all-reduce.11.cloned.1.call-update
  197.9 0.0 all-reduce.13.cloned.1.call-start
  198.0 0.0 copy-done.6
  198.0 39.8 %all-reduce.11.cloned.1.call-done = f32[16,4096]{1,0:T(8,128)} async-done(((f32[16,4096]{1,0:T(8,128)}), f32[16,4096]{1,0:T(8,128)}) %all-reduce.11.cloned.1.call-update) | async-done | bytes 262160 | tf_op jit(solution)/shard_map/psum | solution.py:47
  237.8 1.0 broadcast_multiply_fusion
  238.8 0.0 copy-done
  238.8 11.4 %fusion.3 = f32[128,2048]{1,0:T(8,128)S(1)} fusion(bf16[2048,4096]{1,0:T(8,128)(2,1)} %param.8, f32[112,4096]{1,0:T(8,128)S(1)} %copy-done, f32[16,4096]{1,0:T(8,128)S(1)} %broadcast_multiply_fusion), kind=kOutput, calls=%fused_computation.13 | convolution fusion | flops 2149580800 | bytes 19922944 | tf_op jit(solution)/shard_map/dot_general | solution.py:17
  250.2 134.0 %all-reduce.16 = bf16[128,2048]{1,0:T(8,128)(2,1)} all-reduce(f32[128,2048]{1,0:T(8,128)S(1)} %fusion.3), channel_id=1, replica_groups=mesh['sample'=4,'marker'=32] {'marker'}, use_global_device_ids=true, to_apply=%region_6.0 | all-reduce | flops 262144 | bytes 1572864 | tf_op jit(solution)/shard_map/psum | solution.py:24
  384.2 9.6 %fusion.24 = f32[128,4096]{1,0:T(8,128)} fusion(bf16[128,2048]{1,0:T(8,128)(2,1)} %all-reduce.16, bf16[2048,4096]{1,0:T(8,128)(2,1)} %param.8), kind=kOutput, calls=%fused_computation.52 | convolution fusion | flops 2147483648 | bytes 19398656 | tf_op jit(solution)/shard_map/dot_general | solution.py:29
  393.9 0.0 all-reduce.13.cloned.1.call-update
  393.9 0.0 all-reduce.15.cloned.1.call-start
  394.0 0.1 mul.210
  394.0 0.1 mul.207
  394.1 59.5 %all-reduce.13.cloned.1.call-done = f32[128,4096]{1,0:T(8,128)} async-done(((f32[128,4096]{1,0:T(8,128)}), f32[128,4096]{1,0:T(8,128)}) %all-reduce.13.cloned.1.call-update) | async-done | bytes 2097168 | tf_op jit(solution)/shard_map/psum | solution.py:58
  453.6 2.2 multiply_reduce_fusion.2
  455.8 62.9 %all-reduce.1 = (f32[128]{0:T(128)S(1)}, f32[128]{0:T(128)S(1)}) all-reduce(f32[128]{0:T(128)S(1)} %get-tuple-element.3, f32[128]{0:T(128)S(1)} %get-tuple-element.2), channel_id=1, replica_groups=mesh['sample'=4,'marker'=32] {'marker'}, use_global_device_ids=true, to_apply=%region_5.0 | all-reduce | flops 256 | bytes 2048 | tf_op jit(solution)/shard_map/psum | solution.py:54
  518.7 2.2 multiply_reduce_fusion.1
  520.9 66.8 %psum.91 = f32[128]{0:T(128)S(1)} all-reduce(f32[128]{0:T(128)S(1)} %multiply_reduce_fusion.1), channel_id=1, replica_groups=mesh['sample'=4,'marker'=32] {'marker'}, use_global_device_ids=true, to_apply=%region_11.0 | all-reduce | flops 128 | bytes 1024 | tf_op jit(solution)/shard_map/psum | solution.py:65
  587.7 3.6 multiply_add_fusion.1
  591.3 12.1 %fusion.1 = f32[128,2048]{1,0:T(8,128)S(1)} fusion(bf16[2048,4096]{1,0:T(8,128)(2,1)} %param.8, f32[128,4096]{1,0:T(8,128)} %multiply_add_fusion.1), kind=kOutput, calls=%fused_computation.11 | convolution fusion | flops 2148007936 | bytes 19922944 | tf_op jit(solution)/shard_map/dot_general | solution.py:17
  603.4 129.5 %all-reduce.17 = bf16[128,2048]{1,0:T(8,128)(2,1)} all-reduce(f32[128,2048]{1,0:T(8,128)S(1)} %fusion.1), channel_id=1, replica_groups=mesh['sample'=4,'marker'=32] {'marker'}, use_global_device_ids=true, to_apply=%region_12.0 | all-reduce | flops 262144 | bytes 1572864 | tf_op jit(solution)/shard_map/psum | solution.py:24
  732.9 9.6 %fusion.23 = f32[128,4096]{1,0:T(8,128)} fusion(bf16[128,2048]{1,0:T(8,128)(2,1)} %all-reduce.17, bf16[2048,4096]{1,0:T(8,128)(2,1)} %param.8), kind=kOutput, calls=%fused_computation.51 | convolution fusion | flops 2147483648 | bytes 19398656 | tf_op jit(solution)/shard_map/dot_general | solution.py:29
  742.5 0.0 all-reduce.15.cloned.1.call-update
  742.5 0.1 slice.18
  742.6 0.1 reshape.48
  742.7 58.7 %all-reduce.15.cloned.1.call-done = f32[128,4096]{1,0:T(8,128)} async-done(((f32[128,4096]{1,0:T(8,128)}), f32[128,4096]{1,0:T(8,128)}) %all-reduce.15.cloned.1.call-update) | async-done | bytes 2097168 | tf_op jit(solution)/shard_map/psum | solution.py:58
  801.3 2.7 multiply_reduce_fusion
  804.1 62.9 %psum.94 = f32[128]{0:T(128)S(1)} all-reduce(f32[128]{0:T(128)S(1)} %multiply_reduce_fusion), channel_id=1, replica_groups=mesh['sample'=4,'marker'=32] {'marker'}, use_global_device_ids=true, to_apply=%region_15.0 | all-reduce | flops 128 | bytes 1024 | tf_op jit(solution)/shard_map/psum | solution.py:60
  866.9 2.0 multiply_add_fusion
  868.9 0.0 copy-start.1
  868.9 1.3 copy-done.1
  870.3 0.0 copy-start.4
  870.3 0.0 copy-start.5
  870.3 0.0 copy-start.2
  870.3 0.3 fusion
  870.5 0.1 reshape.47
  870.7 66.8 %psum.95 = f32[16]{0:T(128)S(1)} all-reduce(f32[16]{0:T(128)S(1)} %reduce_sum.78), channel_id=1, replica_groups=mesh['sample'=4,'marker'=32] {'marker'}, use_global_device_ids=true, to_apply=%region_18.0 | all-reduce | flops 16 | bytes 128 | tf_op jit(solution)/shard_map/psum | solution.py:73
  937.5 0.0 copy-done.4
  937.5 0.0 copy-done.5
  937.5 0.0 copy-done.2
  937.5 2.0 fusion.16
  (11 shorter events, 0.1 us)
Async XLA Ops:
  7.2 181.9 %all-reduce.9.cloned.1.call-start = ((), (), s32[]{:S(2)}) async-start(), calls=%async_computation | async-start | bytes 262144 | tf_op jit(solution)/shard_map/psum | solution.py:24
  75.4 113.7 %copy-start.3 = (f32[16,2048]{1,0:T(8,128)S(1)}, f32[16,2048]{1,0:T(8,128)}, u32[]{:S(2)}) copy-start(f32[16,2048]{1,0:T(8,128)} %param.9) | copy-start | bytes 393220
  86.3 111.6 %copy-start.6 = (f32[16]{0:T(128)S(1)}, f32[16]{0:T(128)}, u32[]{:S(2)}) copy-start(f32[16]{0:T(128)} %param.15) | copy-start | bytes 196
  86.3 152.5 %copy-start = (f32[112,4096]{1,0:T(8,128)S(1)}, f32[112,4096]{1,0:T(8,128)}, u32[]{:S(2)}) copy-start(f32[112,4096]{1,0:T(8,128)} %param.11) | copy-start | bytes 5505028
  86.4 151.4 %all-reduce.11.cloned.1.call-start = ((), (), s32[]{:S(2)}) async-start(), calls=%async_computation.1 | async-start | bytes 524288 | tf_op jit(solution)/shard_map/psum | solution.py:47
  197.9 255.7 %all-reduce.13.cloned.1.call-start = ((), (), s32[]{:S(2)}) async-start(), calls=%async_computation.2 | async-start | bytes 4194304 | tf_op jit(solution)/shard_map/psum | solution.py:58
  393.9 407.5 %all-reduce.15.cloned.1.call-start = ((), (), s32[]{:S(2)}) async-start(), calls=%async_computation.3 | async-start | bytes 4194304 | tf_op jit(solution)/shard_map/psum | solution.py:58
  868.9 1.4 copy-start.1
  870.3 67.2 %copy-start.4 = (f32[16]{0:T(128)S(1)}, f32[16]{0:T(128)}, u32[]{:S(2)}) copy-start(f32[16]{0:T(128)} %param.13) | copy-start | bytes 196
  870.3 67.2 %copy-start.5 = (f32[16]{0:T(128)S(1)}, f32[16]{0:T(128)}, u32[]{:S(2)}) copy-start(f32[16]{0:T(128)} %param.14) | copy-start | bytes 196
  870.3 67.2 %copy-start.2 = (f32[16,4096]{1,0:T(8,128)S(1)}, f32[16,4096]{1,0:T(8,128)}, u32[]{:S(2)}) copy-start(f32[16,4096]{1,0:T(8,128)} %param.10) | copy-start | bytes 786436
Sparse Core Ops, SparseCore 0:
  86.5 102.5 all-reduce.8
  198.1 39.6 all-reduce.10
  394.0 59.5 all-reduce.12
  742.6 58.6 all-reduce.14
where the time goes:
time: 947 us; the launch traced here: 946 us
  blocking collectives  587 us (62%)
  waiting for transfers between devices  261 us (28%)
  matrix products  62.4 us (7%)
  other arithmetic  20.5 us (2%)
  between operations  13.9 us (1%)
    psum x2, blocking collectives, project(): predicted = lax.psum(partial_value, 'marker')  264 us
    psum x2, waiting for transfers between devices, per_device(): back_sum = lax.psum(back_sum, 'sample')  118 us
    psum x1, waiting for transfers between devices, project(): predicted = lax.psum(partial_value, 'marker')  103 us
    psum x1, blocking collectives, per_device(): norm_next = lax.psum(jnp.sum(residual * residual, axis=1), 'marker')  66.8 us
    psum x1, blocking collectives, per_device(): probe_dot = lax.psum(probe_local, 'marker')  66.8 us
    psum x1, blocking collectives, per_device(): first_slope = lax.psum(jnp.sum(slopes, axis=1), 'marker') / MARKERS  63.8 us
    psum x1, blocking collectives, per_device(): curvature = lax.psum(jnp.sum(direction * applied, axis=1), 'marker')  62.9 us
    psum x1, blocking collectives, per_device(): norm_start = lax.psum(jnp.sum(residual * residual, axis=1), 'marker')  62.9 us
  transfers between devices with their start and end apart: 4, of which 4 were waited for; matrix products, arithmetic and copies ran while one was open for 0% of the time, Pallas kernels for 0%

commit v1 on v0

v1 whole, which is shorter than its diff:
```python
import functools

import jax
import jax.numpy as jnp
from jax import lax
from jax.experimental import pallas as pl
from jax.experimental.pallas import tpu as pltpu
from jax.sharding import PartitionSpec as P

MESH = pl.DeviceIdType.MESH
F32 = jnp.float32
BF16 = jnp.bfloat16
TRAITS = 16
ROWS = 128
LANES = 128
NT = (((1,), (1,)), ((), ()))


def denoise(signal, precision, shrink, logit_base):
    energy = shrink * precision * signal * signal
    weight = jax.nn.sigmoid(logit_base + 0.5 * energy)
    return shrink * weight * signal, shrink * weight * (1.0 + (1.0 - weight) * energy)


def iota(shape, dim):
    return lax.broadcasted_iota(jnp.int32, shape, dim)


def lane_vector(ref):
    trait = iota((1, LANES), 1) % TRAITS
    value = jnp.zeros((1, LANES), F32)
    for t in range(TRAITS):
        value = jnp.where(trait == t, ref[t], value)
    return value


def to_column(row):
    shape = (TRAITS, LANES)
    picked = jnp.where(iota(shape, 0) == iota(shape, 1), jnp.broadcast_to(row, shape), 0.0)
    return jnp.sum(picked, axis=1, keepdims=True)


def to_row(column):
    shape = (TRAITS, LANES)
    picked = jnp.where(
        iota(shape, 0) == iota(shape, 1) % TRAITS, jnp.broadcast_to(column, shape), 0.0
    )
    return jnp.sum(picked, axis=0, keepdims=True)


def kernel(
    total_people,
    total_markers,
    geno_hbm,
    pheno_hbm,
    message,
    probes_hbm,
    incl,
    slab,
    in_prec,
    noise_prec,
    estimate,
    lmmse,
    geno,
    pheno,
    probes,
    centre,
    v1,
    v2,
    v3,
    slope_out,
    slope_in,
    t1_out,
    t1_in,
    t1_mine,
    t1_all,
    p1_out,
    p1_in,
    p1_mine,
    p1_all,
    t2_out,
    t2_in,
    t2_mine,
    t2_all,
    u_out,
    u_in,
    pm,
    pp,
    acc_t,
    acc_p,
    zt_part,
    zt_a1,
    zt_b1,
    zt_a2,
    zt_b2,
    r0,
    back,
    zp_part,
    zp_a1,
    zp_b1,
    zp_a2,
    zp_b2,
    n0_col,
    q1_col,
    m2_col,
    m3_col,
    mom_out,
    mom_in,
    zmom_out,
    zmom_in,
    geno_sem,
    arg_sem,
    send_t,
    send_p,
    recv_slope,
    recv_t1,
    recv_t1all,
    recv_p1,
    recv_p1all,
    recv_t2,
    recv_t2all,
    recv_u,
    recv_mom,
    zsend,
    zrecv,
):
    people, markers = geno.shape
    group = t1_in.shape[0]
    chunks = geno_sem.shape[0]
    span = people // chunks
    tiles = span // LANES
    owners = 2 * tiles
    me = lax.axis_index("marker")
    zz = lax.axis_index("sample")
    tile, half = me // 2, me % 2
    zsize = zmom_in.shape[0]

    def geno_copy(j):
        rows = pl.ds(pl.multiple_of(j * span, span), span)
        return pltpu.make_async_copy(geno_hbm.at[rows], geno.at[rows], geno_sem.at[j])

    probe_copy = pltpu.make_async_copy(probes_hbm, probes, arg_sem.at[0])
    pheno_copy = pltpu.make_async_copy(pheno_hbm, pheno, arg_sem.at[1])
    probe_copy.start()
    for j in range(chunks):
        geno_copy(j).start()
    pheno_copy.start()

    barrier = pltpu.get_barrier_semaphore()

    @pl.loop(0, group)
    def _(q):
        @pl.when(q != me)
        def _():
            pl.semaphore_signal(barrier, inc=1, device_id={"marker": q}, device_id_type=MESH)

    @pl.loop(1, zsize)
    def _(d):
        pl.semaphore_signal(
            barrier, inc=1, device_id={"sample": (zz + d) % zsize}, device_id_type=MESH
        )

    def remote(src, dst, ssem, rsem, q, axis="marker"):
        return pltpu.make_async_remote_copy(
            src_ref=src,
            dst_ref=dst,
            send_sem=ssem,
            recv_sem=rsem,
            device_id={axis: q},
            device_id_type=MESH,
        )

    def others(body):
        @pl.loop(0, group)
        def _(q):
            @pl.when(q != me)
            def _():
                body(q)

    def scatter_one(out, land, ssem, rsem, q):
        return remote(out.at[q], land.at[me], ssem.at[q], rsem.at[me], q)

    def gather_one(mine, land, ssem, rsem, q):
        return remote(mine, land.at[me], ssem.at[q], rsem.at[me], q)

    def arrivals(land, ssem, rsem):
        others(lambda q: remote(land.at[q], land.at[q], ssem.at[q], rsem.at[q], q).wait_recv())

    def drained(piece, ssem, rsem):
        others(lambda q: remote(piece, piece, ssem.at[q], rsem.at[q], q).wait_send())

    incl_row, slab_row = lane_vector(incl), lane_vector(slab)
    prec_row, noise_row = lane_vector(in_prec), lane_vector(noise_prec)
    shrink_row = slab_row / (1.0 + slab_row)
    odds_row = jnp.log(incl_row / (1.0 - incl_row))
    base_row = odds_row + 0.5 * jnp.log(1.0 - shrink_row)
    scale_row = noise_row / total_people
    shrink_c, base_c, prec_c = to_column(shrink_row), to_column(base_row), to_column(prec_row)
    scale_c = to_column(scale_row)

    width = min(512, markers)

    def columns(i):
        return pl.ds(pl.multiple_of(i * width, width), width)

    def slope_step(i, total):
        return total + denoise(message[:, columns(i)], prec_c, shrink_c, base_c)[1]

    slopes = lax.fori_loop(0, markers // width, slope_step, jnp.zeros((TRAITS, width), F32))
    slope_out[...] = to_row(jnp.sum(slopes, axis=1, keepdims=True))

    pl.semaphore_wait(barrier, group - 1 + zsize - 1)

    others(lambda q: gather_one(slope_out, slope_in, send_t, recv_slope, q).start())
    slope_in[me] = slope_out[...]

    n0_col[...] = jnp.zeros_like(n0_col)
    q1_col[...] = jnp.zeros_like(q1_col)
    m2_col[...] = jnp.zeros_like(m2_col)
    m3_col[...] = jnp.zeros_like(m3_col)
    probe_copy.wait()

    @pl.loop(0, ROWS // TRAITS - 1)
    def _(k):
        rows = pl.ds(pl.multiple_of(k * TRAITS, TRAITS), TRAITS)
        below = pl.ds(pl.multiple_of(k * TRAITS + TRAITS, TRAITS), TRAITS)

        def step(i, total):
            part = probes[rows, columns(i)]
            v1[below, columns(i)] = part.astype(BF16)
            return total + part * part

        squares = lax.fori_loop(0, markers // width, step, jnp.zeros((TRAITS, width), F32))
        n0_col[below, :] = jnp.sum(squares, axis=1, keepdims=True)

    arrivals(slope_in, send_t, recv_slope)
    slope_row = jnp.sum(slope_in[...], axis=0) / total_markers
    lam_row = prec_row * (1.0 - slope_row) / slope_row
    slope_c = to_column(slope_row)

    @pl.loop(0, markers // width)
    def _(i):
        signal = message[:, columns(i)]
        first = denoise(signal, prec_c, shrink_c, base_c)[0]
        value = (first - slope_c * signal) / (1.0 - slope_c)
        centre[:, columns(i)] = value
        v1[:TRAITS, columns(i)] = value.astype(BF16)

    drained(slope_out, send_t, recv_slope)

    def rows_of(j):
        return pl.ds(pl.multiple_of(j * span, span), span)

    def put_traits(out, value, j):
        for i in range(tiles):
            for h in range(2):
                out[j * owners + 2 * i + h] = value[
                    8 * h : 8 * h + 8, LANES * i : LANES * i + LANES
                ]

    def put_rows(out, value, j):
        for i in range(tiles):
            for h in range(2):
                out[j * owners + 2 * i + h] = value[
                    64 * h : 64 * h + 64, LANES * i : LANES * i + LANES
                ].astype(BF16)

    def scatter_chunk(j, out, land, ssem, rsem):
        @pl.loop(0, owners)
        def _(i):
            q = j * owners + i

            @pl.when(q != me)
            def _():
                scatter_one(out, land, ssem, rsem, q).start()

    @pl.loop(0, chunks)
    def _(j):
        geno_copy(j).wait()
        value = lax.dot_general(v1[...], geno[rows_of(j), :], NT, preferred_element_type=F32)
        put_traits(t1_out, value[:TRAITS], j)
        scatter_chunk(j, t1_out, t1_in, send_t, recv_t1)
        put_rows(p1_out, value, j)
        scatter_chunk(j, p1_out, p1_in, send_p, recv_p1)

    trait_rows = pl.ds(pl.multiple_of(half * 8, 8), 8)
    wide_rows = pl.ds(pl.multiple_of(half * 64, 64), 64)
    tile_cols = pl.ds(pl.multiple_of(tile * LANES, LANES), LANES)

    t1_in[me] = t1_out[me]
    p1_in[me] = p1_out[me]
    pheno_copy.wait()
    arrivals(t1_in, send_t, recv_t1)
    drained(t1_out.at[0], send_t, recv_t1)
    t1_mine[...] = pheno[trait_rows, tile_cols] - jnp.sum(t1_in[...], axis=0)
    others(lambda q: gather_one(t1_mine, t1_all, send_t, recv_t1all, q).start())
    t1_all[me] = t1_mine[...]

    def summed(land):
        def step(q, total):
            return total + land[q].astype(F32)

        return lax.fori_loop(0, group, step, jnp.zeros((64, LANES), F32))

    arrivals(p1_in, send_p, recv_p1)
    drained(p1_out.at[0], send_p, recv_p1)
    p1_mine[...] = summed(p1_in).astype(BF16)
    others(lambda q: gather_one(p1_mine, p1_all, send_p, recv_p1all, q).start())
    p1_all[me] = p1_mine[...]
    widened = p1_mine[...].astype(F32)
    q1_col[wide_rows, :] = jnp.sum(widened * widened, axis=1, keepdims=True)
    q1_col[:TRAITS, :] = jnp.zeros((TRAITS, 1), F32)

    def join_traits(land):
        @pl.loop(0, people // LANES)
        def _(t):
            cols = pl.ds(pl.multiple_of(t * LANES, LANES), LANES)
            pm[:, cols] = jnp.concatenate([land[2 * t], land[2 * t + 1]], axis=0).astype(BF16)

    def back_traits():
        zt_part[...] = jnp.dot(pm[:, :span], geno[:span, :], preferred_element_type=F32)

        @pl.loop(1, chunks)
        def _(j):
            zt_part[...] += jnp.dot(
                pm[:, rows_of(j)], geno[rows_of(j), :], preferred_element_type=F32
            )

    arrivals(t1_all, send_t, recv_t1all)
    drained(t1_mine, send_t, recv_t1all)
    join_traits(t1_all)
    back_traits()

    pair = zz + 1 - 2 * (zz % 2)
    cross = (zz + zsize - 1 + 2 * (zz % 2)) % zsize
    quarter = markers // 8
    keep_a = ((zz + 1) // 2) % 2
    keep_b = zz // 2
    last = zz % 2
    two = 2 * quarter

    def cols_at(start, size):
        return pl.ds(pl.multiple_of(start, quarter), size)

    own_a, give_a = cols_at(keep_a * two, two), cols_at((1 - keep_a) * two, two)
    own_b = cols_at(2 * two + keep_b * two, two)
    give_b = cols_at(2 * two + (1 - keep_b) * two, two)
    q_own_a = cols_at(keep_a * two + last * quarter, quarter)
    q_give_a = cols_at(keep_a * two + (1 - last) * quarter, quarter)
    q_own_b = cols_at(2 * two + keep_b * two + last * quarter, quarter)
    q_give_b = cols_at(2 * two + keep_b * two + (1 - last) * quarter, quarter)

    def zcopy(src, dst, k, q):
        return remote(src, dst, zsend.at[k], zrecv.at[k], q, "sample")

    def zphase(k, part, a1, b1, a2, b2, full):
        first = (
            zcopy(part.at[:, give_a], a1, k, pair),
            zcopy(part.at[:, give_b], b1, k + 1, cross),
        )
        second = (
            zcopy(part.at[:, q_give_a], a2, k + 2, cross),
            zcopy(part.at[:, q_give_b], b2, k + 3, pair),
        )
        third = (
            zcopy(full.at[:, q_own_a], full.at[:, q_own_a], k + 4, cross),
            zcopy(full.at[:, q_own_b], full.at[:, q_own_b], k + 5, pair),
        )
        fourth = (
            zcopy(full.at[:, own_a], full.at[:, own_a], k + 6, pair),
            zcopy(full.at[:, own_b], full.at[:, own_b], k + 7, cross),
        )
        return first, second, third, fourth

    def start(copies):
        for copy in copies:
            copy.start()

    def finish(copies):
        for copy in copies:
            copy.wait()

    def add_into(part, cols, extra):
        total = part[:, cols].astype(F32) + extra[...].astype(F32)
        part[:, cols] = total.astype(part.dtype)

    def zstep1(steps, part, a1, b1, a2, b2, full):
        finish(steps[0])
        add_into(part, own_a, a1)
        add_into(part, own_b, b1)
        start(steps[1])

    def zstep2(steps, part, a1, b1, a2, b2, full):
        finish(steps[1])
        for cols, extra in ((q_own_a, a2), (q_own_b, b2)):
            total = part[:, cols].astype(F32) + extra[...].astype(F32)
            full[:, cols] = total.astype(full.dtype)
        start(steps[2])

    def zstep3(steps):
        finish(steps[2])
        start(steps[3])

    t_args = (zt_part, zt_a1, zt_b1, zt_a2, zt_b2, r0)
    t_steps = zphase(0, *t_args)
    start(t_steps[0])

    arrivals(p1_all, send_p, recv_p1all)
    drained(p1_mine, send_p, recv_p1all)

    @pl.loop(0, people // LANES)
    def _(t):
        cols = pl.ds(pl.multiple_of(t * LANES, LANES), LANES)
        pp[:64, cols] = p1_all[2 * t]
        pp[64:, cols] = p1_all[2 * t + 1]

    acc_p[...] = jnp.zeros_like(acc_p)

    def back_probes(lo, hi):
        @pl.loop(lo, hi)
        def _(j):
            acc_p[...] += jnp.dot(
                pp[:, rows_of(j)], geno[rows_of(j), :], preferred_element_type=F32
            )

    mid = (chunks + 1) // 2
    back_probes(0, mid)
    zstep1(t_steps, *t_args)
    back_probes(mid, chunks)

    @pl.loop(0, markers // width)
    def _(i):
        zp_part[:, columns(i)] = acc_p[TRAITS:, columns(i)].astype(BF16)

    zstep2(t_steps, *t_args)
    v3p = v3.at[pl.ds(TRAITS, ROWS - TRAITS)]
    p_args = (zp_part, zp_a1, zp_b1, zp_a2, zp_b2, v3p)
    p_steps = zphase(8, *p_args)
    zstep3(t_steps)
    start(p_steps[0])
    finish(t_steps[3])

    def residual_step(i, total):
        value = scale_c * r0[:, columns(i)]
        centre_free = value
        v2[:, columns(i)] = centre_free.astype(BF16)
        return total + value * value

    squares = lax.fori_loop(0, markers // width, residual_step, jnp.zeros((TRAITS, width), F32))
    n0_col[:TRAITS, :] = jnp.sum(squares, axis=1, keepdims=True)

    def second_project(lo, hi):
        @pl.loop(lo, hi)
        def _(j):
            value = lax.dot_general(v2[...], geno[rows_of(j), :], NT, preferred_element_type=F32)
            put_traits(t2_out, value, j)
            scatter_chunk(j, t2_out, t2_in, send_t, recv_t2)

    second_project(0, chunks)
    zstep1(p_steps, *p_args)
    t2_in[me] = t2_out[me]
    arrivals(t2_in, send_t, recv_t2)
    drained(t2_out.at[0], send_t, recv_t2)
    rounded = jnp.sum(t2_in[...], axis=0).astype(BF16).astype(F32)
    t2_mine[...] = rounded
    others(lambda q: gather_one(t2_mine, t2_all, send_t, recv_t2all, q).start())
    t2_all[me] = t2_mine[...]
    q1_col[trait_rows, :] = jnp.sum(rounded * rounded, axis=1, keepdims=True)
    zstep2(p_steps, *p_args)
    arrivals(t2_all, send_t, recv_t2all)
    drained(t2_mine, send_t, recv_t2all)
    join_traits(t2_all)
    back_traits2 = (acc_t, zt_a1, zt_b1, zt_a2, zt_b2, back)

    acc_t[...] = jnp.dot(pm[:, :span], geno[:span, :], preferred_element_type=F32)

    @pl.loop(1, chunks)
    def _(j):
        acc_t[...] += jnp.dot(pm[:, rows_of(j)], geno[rows_of(j), :], preferred_element_type=F32)

    s_steps = zphase(16, *back_traits2)
    start(s_steps[0])
    zstep3(p_steps)
    zstep1(s_steps, *back_traits2)
    zstep2(s_steps, *back_traits2)
    zstep3(s_steps)
    finish(p_steps[3])
    finish(s_steps[3])

    @pl.loop(0, markers // width)
    def _(i):
        v3[:TRAITS, columns(i)] = back[:, columns(i)].astype(BF16)

    @pl.loop(0, chunks)
    def _(j):
        value = lax.dot_general(v3[...], geno[rows_of(j), :], NT, preferred_element_type=F32)
        put_rows(u_out, value, j)
        scatter_chunk(j, u_out, u_in, send_p, recv_u)

    u_in[me] = u_out[me]
    arrivals(u_in, send_p, recv_u)
    drained(u_out.at[0], send_p, recv_u)
    u = summed(u_in)
    mine = p1_mine[...].astype(F32)
    top = jnp.concatenate([t2_all[2 * tile], t2_all[2 * tile + 1]], axis=0)
    mine = jnp.concatenate([jnp.where(half == 0, top, mine[:TRAITS]), mine[TRAITS:]], axis=0)
    m2_col[wide_rows, :] = jnp.sum(u * mine, axis=1, keepdims=True)
    m3_col[wide_rows, :] = jnp.sum(u * u, axis=1, keepdims=True)

    lane = iota((ROWS, LANES), 1)
    moments = jnp.where(lane == 0, n0_col[...] * (1.0 / zsize), 0.0)
    moments = jnp.where(lane == 1, q1_col[...], moments)
    moments = jnp.where(lane == 2, m2_col[...], moments)
    moments = jnp.where(lane == 3, m3_col[...], moments)
    mom_out[...] = jnp.transpose(moments)[:8]
    others(lambda q: gather_one(mom_out, mom_in, send_t, recv_mom, q).start())
    mom_in[me] = mom_out[...]
    arrivals(mom_in, send_t, recv_mom)
    drained(mom_out, send_t, recv_mom)
    zmom_out[...] = jnp.sum(mom_in[...], axis=0)

    def zmom(d):
        q = (zz + d) % zsize
        return zcopy(zmom_out, zmom_in.at[d], 24 + d, q)

    for d in range(1, zsize):
        zmom(d).start()
    zmom_in[0] = zmom_out[...]
    for d in range(1, zsize):
        zmom(d).wait()
    totals = jnp.zeros((8, LANES), F32)
    for q in range(zsize):
        totals = totals + zmom_in[(zz + zsize - q) % zsize]

    n0, q1, m2, m3 = totals[0:1], totals[1:2], totals[2:3], totals[3:4]
    step1 = n0 / (scale_row * q1 + lam_row * n0)
    shrunk = 1.0 - step1 * lam_row
    gain = step1 * scale_row
    n1 = shrunk * shrunk * n0 - 2.0 * shrunk * gain * q1 + gain * gain * m2
    beta = n1 / n0
    mix = shrunk + beta
    p2 = mix * mix * q1 - 2.0 * mix * gain * m2 + gain * gain * m3
    step2 = n1 / (scale_row * p2 + lam_row * (n1 + beta * beta * n0))
    is_probe = iota((1, LANES), 1) >= TRAITS
    dot_row = jnp.where(is_probe, step1 * n0 + step2 * n1, 0.0)
    norm_row = jnp.where(is_probe, n0, 0.0)
    for shift in (16, 32, 64):
        dot_row = dot_row + pltpu.roll(dot_row, shift, 1)
        norm_row = norm_row + pltpu.roll(norm_row, shift, 1)
    eta = lam_row * dot_row / (norm_row + 1e-6)
    next_prec = lam_row * (1.0 - eta) / eta
    slab_var = slab_row / prec_row
    next_shrink = slab_var * next_prec / (1.0 + slab_var * next_prec)
    next_base = odds_row + 0.5 * jnp.log(1.0 - next_shrink)

    along_r = to_column((step1 + step2 * mix) * scale_row)
    along_b = to_column(step2 * gain)
    eta_c, prec2_c = to_column(eta), to_column(next_prec)
    shrink2_c, base2_c = to_column(next_shrink), to_column(next_base)

    @pl.loop(0, markers // width)
    def _(i):
        middle = centre[:, columns(i)]
        found = middle + along_r * r0[:, columns(i)] - along_b * back[:, columns(i)]
        lmmse[:, columns(i)] = found
        signal = (found - eta_c * middle) / (1.0 - eta_c)
        estimate[:, columns(i)] = denoise(signal, prec2_c, shrink2_c, base2_c)[0]


def per_device(
    genotypes, phenotypes, message, probes, inclusion, slab_ratio, input_precision, noise_precision
):
    people, markers = genotypes.shape
    zsize, group = lax.axis_size("sample"), lax.axis_size("marker")
    assert group == 2 * people // LANES and zsize == 4
    assert message.shape[0] == TRAITS and probes.shape[0] == ROWS - TRAITS
    chunks = max(1, people // 512)
    rest = ROWS - TRAITS
    quarter = markers // 8
    vmem = pltpu.VMEM
    dma = pltpu.SemaphoreType.DMA
    piece_t = vmem((group, 8, LANES), F32)
    piece_p = vmem((group, 64, LANES), BF16)
    whole = pl.BlockSpec(memory_space=pltpu.VMEM)
    far = pl.BlockSpec(memory_space=pl.ANY)
    scalars = pl.BlockSpec(memory_space=pltpu.SMEM)
    out = jax.ShapeDtypeStruct((TRAITS, markers), F32)
    return pl.pallas_call(
        functools.partial(kernel, float(people * zsize), float(markers * group)),
        out_shape=(out, out),
        in_specs=[far, far, whole, far, scalars, scalars, scalars, scalars],
        out_specs=(whole, whole),
        scratch_shapes=[
            vmem((people, markers), BF16),
            vmem((TRAITS, people), F32),
            vmem((rest, markers), F32),
            vmem((TRAITS, markers), F32),
            vmem((ROWS, markers), BF16),
            vmem((TRAITS, markers), BF16),
            vmem((ROWS, markers), BF16),
            vmem((1, LANES), F32),
            vmem((group, 1, LANES), F32),
            piece_t,
            piece_t,
            vmem((8, LANES), F32),
            piece_t,
            piece_p,
            piece_p,
            vmem((64, LANES), BF16),
            piece_p,
            piece_t,
            piece_t,
            vmem((8, LANES), F32),
            piece_t,
            piece_p,
            piece_p,
            vmem((TRAITS, people), BF16),
            vmem((ROWS, people), BF16),
            vmem((TRAITS, markers), F32),
            vmem((ROWS, markers), F32),
            vmem((TRAITS, markers), F32),
            vmem((TRAITS, 2 * quarter), F32),
            vmem((TRAITS, 2 * quarter), F32),
            vmem((TRAITS, quarter), F32),
            vmem((TRAITS, quarter), F32),
            vmem((TRAITS, markers), F32),
            vmem((TRAITS, markers), F32),
            vmem((rest, markers), BF16),
            vmem((rest, 2 * quarter), BF16),
            vmem((rest, 2 * quarter), BF16),
            vmem((rest, quarter), BF16),
            vmem((rest, quarter), BF16),
            vmem((ROWS, 1), F32),
            vmem((ROWS, 1), F32),
            vmem((ROWS, 1), F32),
            vmem((ROWS, 1), F32),
            vmem((8, LANES), F32),
            vmem((group, 8, LANES), F32),
            vmem((8, LANES), F32),
            vmem((zsize, 8, LANES), F32),
            dma((chunks,)),
            dma((2,)),
            dma((group,)),
            dma((group,)),
            dma((group,)),
            dma((group,)),
            dma((group,)),
            dma((group,)),
            dma((group,)),
            dma((group,)),
            dma((group,)),
            dma((group,)),
            dma((group,)),
            dma((24 + zsize,)),
            dma((24 + zsize,)),
        ],
        compiler_params=pltpu.CompilerParams(
            collective_id=0, has_side_effects=True, vmem_limit_bytes=60 << 20
        ),
        name="vamp_round",
    )(
        genotypes,
        phenotypes,
        message,
        probes,
        inclusion,
        slab_ratio,
        input_precision,
        noise_precision,
    )


def solution(mesh):
    return jax.shard_map(
        per_device,
        mesh=mesh,
        in_specs=(
            P("sample", "marker"),
            P(None, "sample"),
            P(None, "marker"),
            P(None, "marker"),
            P(),
            P(),
            P(),
            P(),
        ),
        out_specs=(P(None, "marker"), P(None, "marker")),
        check_vma=False,
    )
```

time: 947 us -> 121 us (0.13)
  blocking collectives: 587 us -> 0 us
  waiting for transfers between devices: 261 us -> 0 us
  Pallas kernels: 0 us -> 117 us
  matrix products: 62.4 us -> 0 us
  other arithmetic: 20.5 us -> 0 us
  between operations: 13.9 us -> 0.64 us
    psum x7 -> x0, blocking collectives: 587 us -> none  [the longest x2 264 us: project(): predicted = lax.psum(partial_value, 'marker')]
    psum x4 -> x0, waiting for transfers between devices: 261 us -> none  [the longest x2 118 us: per_device(): back_sum = lax.psum(back_sum, 'sample')]
    pallas_call x0 -> x1, Pallas kernels: none -> 117 us  [per_device(): pl.pallas_call(functools.partial(kernel, float(people * zsize), float(mar...]
    dot_general x6 -> x0, matrix products: 62.4 us -> none  [the longest x3 34.3 us: contract_rows(): lax.dot_general(vectors, genotypes, (((1,), (1,)), ((), ())), preferred_e...]
  transfers between devices with their start and end apart: 4 -> 0, of which waited for: 4 -> 0; matrix products, arithmetic and copies ran while one was open for 0% -> 0% of each run, Pallas kernels for 0% -> 0%
where the time goes in v1:
time: 121 us
  Pallas kernels  117 us (97%)
  local copies, waits for them, and re-layouts  3.34 us (3%)
    pallas_call x1, Pallas kernels, per_device(): pl.pallas_call(functools.partial(kernel, float(people * zsize), float(mar...  117 us
    unnamed x2, local copies, waits for them, and re-layouts  3.34 us

profile of v1, /device:TPU:1, one launch (start us, length us, event | category | flops | bytes accessed | tf_op | source)
XLA Modules:
  0.0 120.8 jit_solution(6579834835453796685)
XLA Ops:
  0.6 116.8 %vamp_round.1 = (f32[16,4096]{1,0:T(8,128)}, f32[16,4096]{1,0:T(8,128)}) custom-call(bf16[2048,4096]{1,0:T(8,128)(2,1)} %geno_hbm.1, f32[16,2048]{1,0:T(8,128)} %pheno_hbm.1, f32[16,4096]{1,0:T(8,128)} %message.1, f32[112,4096]{1,0:T(8,128)} %probes_hbm.1, f32[16]{0:T(128)} %incl.1, f32[16]{0:T(128)} %slab.1, f32[16]{0:T(128)} %in_prec.1, f32[16]{0:T(128)} %noise_prec.1), custom_call_target="tpu_custom_call" | custom-call | tf_op jit(solution)/shard_map/vamp_round/pallas_call | solution.py:588
  117.5 1.7 %copy.12 = f32[16,4096]{1,0:T(8,128)} copy(f32[16,4096]{1,0:T(8,128)} %get-tuple-element.4) | data formatting | bytes 524288
  119.2 1.7 %copy.13 = f32[16,4096]{1,0:T(8,128)} copy(f32[16,4096]{1,0:T(8,128)} %get-tuple-element.5) | data formatting | bytes 524288

commit v2 on v1

v2 whole, which is shorter than its diff:
```python
import functools

import jax
import jax.numpy as jnp
from jax import lax
from jax.experimental import pallas as pl
from jax.experimental.pallas import tpu as pltpu
from jax.sharding import PartitionSpec as P

MESH = pl.DeviceIdType.MESH
F32 = jnp.float32
BF16 = jnp.bfloat16
TRAITS = 16
ROWS = 128
LANES = 128
NT = (((1,), (1,)), ((), ()))


def denoise(signal, precision, shrink, logit_base):
    energy = shrink * precision * signal * signal
    weight = jax.nn.sigmoid(logit_base + 0.5 * energy)
    return shrink * weight * signal, shrink * weight * (1.0 + (1.0 - weight) * energy)


def iota(shape, dim):
    return lax.broadcasted_iota(jnp.int32, shape, dim)


def lane_vector(ref):
    trait = iota((1, LANES), 1) % TRAITS
    value = jnp.zeros((1, LANES), F32)
    for t in range(TRAITS):
        value = jnp.where(trait == t, ref[t], value)
    return value


def to_column(row):
    shape = (TRAITS, LANES)
    picked = jnp.where(iota(shape, 0) == iota(shape, 1), jnp.broadcast_to(row, shape), 0.0)
    return jnp.sum(picked, axis=1, keepdims=True)


def to_row(column):
    shape = (TRAITS, LANES)
    picked = jnp.where(
        iota(shape, 0) == iota(shape, 1) % TRAITS, jnp.broadcast_to(column, shape), 0.0
    )
    return jnp.sum(picked, axis=0, keepdims=True)


def kernel(
    total_people,
    total_markers,
    geno_hbm,
    pheno_hbm,
    message_hbm,
    probes_hbm,
    incl,
    slab,
    in_prec,
    noise_prec,
    centre,
    r0,
    back,
    coefs,
    geno,
    pheno,
    message,
    probes,
    v1,
    v2,
    v3,
    slope_out,
    slope_in,
    raw,
    t1_out,
    t1_in,
    t1_mine,
    t1_all,
    p1_out,
    p1_in,
    p1_mine,
    p1_all,
    t2_out,
    t2_in,
    t2_mine,
    t2_all,
    u_out,
    u_in,
    pm,
    pp,
    acc_p,
    exact,
    exact_in1,
    exact_mid,
    exact_in2,
    zt,
    zs,
    zp_part,
    zp_a1,
    zp_b1,
    zp_a2,
    zp_b2,
    n0_col,
    q1_col,
    m2_col,
    m3_col,
    mom_out,
    mom_in,
    zmom_out,
    zmom_in,
    geno_sem,
    arg_sem,
    send_sem,
    recv_sem,
    t1_sem,
    t2_sem,
    zsend,
    zrecv,
):
    people, markers = geno.shape
    group = t1_in.shape[0]
    chunks = geno_sem.shape[0]
    span = people // chunks
    tiles = span // LANES
    owners = 2 * tiles
    me = lax.axis_index("marker")
    zz = lax.axis_index("sample")
    tile, half = me // 2, me % 2
    zsize = zmom_in.shape[0]
    SLOPE, T1, P1, T1ALL, P1ALL, T2, T2ALL, U, MOM = range(9)

    def geno_copy(j):
        rows = pl.ds(pl.multiple_of(j * span, span), span)
        return pltpu.make_async_copy(geno_hbm.at[rows], geno.at[rows], geno_sem.at[j])

    message_copy = pltpu.make_async_copy(message_hbm, message, arg_sem.at[2])
    probe_copy = pltpu.make_async_copy(probes_hbm, probes, arg_sem.at[0])
    pheno_copy = pltpu.make_async_copy(pheno_hbm, pheno, arg_sem.at[1])
    message_copy.start()
    probe_copy.start()
    for j in range(chunks):
        geno_copy(j).start()
    pheno_copy.start()

    barrier = pltpu.get_barrier_semaphore()

    @pl.loop(0, group)
    def _(q):
        @pl.when(q != me)
        def _():
            pl.semaphore_signal(barrier, inc=1, device_id={"marker": q}, device_id_type=MESH)

    @pl.loop(1, zsize)
    def _(d):
        pl.semaphore_signal(
            barrier, inc=1, device_id={"sample": (zz + d) % zsize}, device_id_type=MESH
        )

    def remote(src, dst, ssem, rsem, q, axis="marker"):
        return pltpu.make_async_remote_copy(
            src_ref=src,
            dst_ref=dst,
            send_sem=ssem,
            recv_sem=rsem,
            device_id={axis: q},
            device_id_type=MESH,
        )

    def others(body):
        @pl.loop(0, group)
        def _(q):
            @pl.when(q != me)
            def _():
                body(q)

    def scatter_one(k, out, land, q):
        return remote(out.at[q], land.at[me], send_sem.at[k], recv_sem.at[k], q)

    def gather_all(k, mine, land, sem=None):
        sem = recv_sem.at[k] if sem is None else sem
        others(lambda q: remote(mine, land.at[me], send_sem.at[k], sem, q).start())

    def bulk(k, land, count, sem=None):
        part = land.at[pl.ds(0, count)]
        sem = recv_sem.at[k] if sem is None else sem
        return remote(part, part, send_sem.at[k], sem, (me + 1) % group)

    def arrived(k, land):
        bulk(k, land, group - 1).wait_recv()

    def drained(k, land):
        bulk(k, land, group - 1).wait_send()

    incl_row, slab_row = lane_vector(incl), lane_vector(slab)
    prec_row, noise_row = lane_vector(in_prec), lane_vector(noise_prec)
    shrink_row = slab_row / (1.0 + slab_row)
    odds_row = jnp.log(incl_row / (1.0 - incl_row))
    base_row = odds_row + 0.5 * jnp.log(1.0 - shrink_row)
    scale_row = noise_row / total_people
    shrink_c, base_c, prec_c = to_column(shrink_row), to_column(base_row), to_column(prec_row)
    scale_c = to_column(scale_row)

    width = min(512, markers)
    steps = markers // width

    def columns(i):
        return pl.ds(pl.multiple_of(i * width, width), width)

    def split(rows, i, value):
        high = value.astype(BF16)
        v1[rows : rows + TRAITS, columns(i)] = high
        v1[rows + TRAITS : rows + 2 * TRAITS, columns(i)] = (value - high.astype(F32)).astype(BF16)

    def slope_step(i, total):
        signal = message[:, columns(i)]
        first, slope = denoise(signal, prec_c, shrink_c, base_c)
        centre[:, columns(i)] = first
        split(0, i, first)
        split(2 * TRAITS, i, signal)
        return total + slope

    message_copy.wait()
    slopes = lax.fori_loop(0, steps, slope_step, jnp.zeros((TRAITS, width), F32))
    slope_out[...] = to_row(jnp.sum(slopes, axis=1, keepdims=True))

    pl.semaphore_wait(barrier, group - 1 + zsize - 1)

    gather_all(SLOPE, slope_out, slope_in)
    slope_in[me] = slope_out[...]

    n0_col[...] = jnp.zeros_like(n0_col)
    q1_col[...] = jnp.zeros_like(q1_col)
    m2_col[...] = jnp.zeros_like(m2_col)
    m3_col[...] = jnp.zeros_like(m3_col)
    probe_copy.wait()

    @pl.loop(0, ROWS // TRAITS - 1)
    def _(k):
        rows = pl.ds(pl.multiple_of(k * TRAITS, TRAITS), TRAITS)
        below = pl.ds(pl.multiple_of(k * TRAITS + TRAITS, TRAITS), TRAITS)
        stacked = pl.ds(pl.multiple_of(k * TRAITS + 4 * TRAITS, TRAITS), TRAITS)

        def step(i, total):
            part = probes[rows, columns(i)]
            v1[stacked, columns(i)] = part.astype(BF16)
            return total + part * part

        squares = lax.fori_loop(0, steps, step, jnp.zeros((TRAITS, width), F32))
        n0_col[below, :] = jnp.sum(squares, axis=1, keepdims=True)

    def rows_of(j):
        return pl.ds(pl.multiple_of(j * span, span), span)

    def put_traits(out, value, j):
        for i in range(tiles):
            for h in range(2):
                out[j * owners + 2 * i + h] = value[
                    8 * h : 8 * h + 8, LANES * i : LANES * i + LANES
                ]

    def put_rows(out, value, j):
        for i in range(tiles):
            for h in range(2):
                out[j * owners + 2 * i + h] = value[
                    64 * h : 64 * h + 64, LANES * i : LANES * i + LANES
                ].astype(BF16)

    def scatter_chunk(k, j, out, land):
        @pl.loop(0, owners)
        def _(i):
            q = j * owners + i

            @pl.when(q != me)
            def _():
                scatter_one(k, out, land, q).start()

    @pl.loop(0, chunks)
    def _(j):
        geno_copy(j).wait()
        value = lax.dot_general(v1[...], geno[rows_of(j), :], NT, preferred_element_type=F32)
        raw[:, rows_of(j)] = value[: 4 * TRAITS]
        put_rows(p1_out, value[3 * TRAITS :], j)
        scatter_chunk(P1, j, p1_out, p1_in)

    arrived(SLOPE, slope_in)
    slope_row = jnp.sum(slope_in[...], axis=0) / total_markers
    lam_row = prec_row * (1.0 - slope_row) / slope_row
    slope_c = to_column(slope_row)

    @pl.loop(0, chunks)
    def _(j):
        part = raw[:, rows_of(j)]
        first = part[:TRAITS] + part[TRAITS : 2 * TRAITS]
        signal = part[2 * TRAITS : 3 * TRAITS] + part[3 * TRAITS :]
        put_traits(t1_out, (first - slope_c * signal) / (1.0 - slope_c), j)
        scatter_chunk(T1, j, t1_out, t1_in)

    drained(SLOPE, slope_in)
    trait_rows = pl.ds(pl.multiple_of(half * 8, 8), 8)
    wide_rows = pl.ds(pl.multiple_of(half * 64, 64), 64)
    tile_cols = pl.ds(pl.multiple_of(tile * LANES, LANES), LANES)

    @pl.loop(0, steps)
    def _(i):
        centre[:, columns(i)] = (centre[:, columns(i)] - slope_c * message[:, columns(i)]) / (
            1.0 - slope_c
        )

    t1_in[me] = t1_out[me]
    p1_in[me] = p1_out[me]
    pheno_copy.wait()

    arrived(T1, t1_in)
    t1_mine[...] = (pheno[trait_rows, tile_cols] - jnp.sum(t1_in[...], axis=0)).astype(BF16)
    gather_all(T1ALL, t1_mine, t1_all, t1_sem.at[me // owners])
    t1_all[me] = t1_mine[...]

    def summed(land):
        def step(q, total):
            return total + land[q].astype(F32)

        return lax.fori_loop(0, group, step, jnp.zeros((64, LANES), F32))

    arrived(P1, p1_in)
    p1_mine[...] = summed(p1_in).astype(BF16)
    gather_all(P1ALL, p1_mine, p1_all)
    p1_all[me] = p1_mine[...]
    widened = p1_mine[...].astype(F32)
    q1_col[wide_rows, :] = jnp.sum(widened * widened, axis=1, keepdims=True)
    q1_col[:TRAITS, :] = jnp.zeros((TRAITS, 1), F32)
    drained(T1, t1_in)
    drained(P1, p1_in)

    def back_traits(k, land, sems, rows):
        @pl.loop(0, chunks)
        def _(j):
            mine = me // owners == j

            @pl.when(mine)
            def _():
                bulk(k, land, owners - 1, sems.at[j]).wait_recv()

            @pl.when(jnp.logical_not(mine))
            def _():
                bulk(k, land, owners, sems.at[j]).wait_recv()

            @pl.loop(0, tiles)
            def _(i):
                t = j * tiles + i
                cols = pl.ds(pl.multiple_of(t * LANES, LANES), LANES)
                pm[:8, cols] = land[2 * t]
                pm[8:, cols] = land[2 * t + 1]

            part = jnp.dot(pm[:, rows_of(j)], geno[rows_of(j), :], preferred_element_type=F32)

            @pl.when(j == 0)
            def _():
                exact[rows, :] = part

            @pl.when(j > 0)
            def _():
                exact[rows, :] += part

        drained(k, land)

    top, low = pl.ds(0, TRAITS), pl.ds(TRAITS, TRAITS)
    back_traits(T1ALL, t1_all, t1_sem, top)

    pair = zz + 1 - 2 * (zz % 2)
    cross = (zz + zsize - 1 + 2 * (zz % 2)) % zsize
    quarter = markers // 8
    two = 2 * quarter

    def zcopy(src, dst, k, q):
        return remote(src, dst, zsend.at[k], zrecv.at[k], q, "sample")

    def start(copies):
        for copy in copies:
            copy.start()

    def finish(copies):
        for copy in copies:
            copy.wait()

    left, right = pl.ds(0, markers // 2), pl.ds(markers // 2, markers // 2)

    def doubling(k, out1, in1, out2, in2):
        return (
            (
                zcopy(out1.at[:, left], in1.at[:, left], k, pair),
                zcopy(out1.at[:, right], in1.at[:, right], k + 1, cross),
            ),
            (
                zcopy(out2.at[:, left], in2.at[:, left], k + 2, cross),
                zcopy(out2.at[:, right], in2.at[:, right], k + 3, pair),
            ),
        )

    def rounded_start(hops, z, rows):
        z[0] = exact[rows, :].astype(BF16)
        start(hops[0])

    def rounded_middle(hops, z):
        finish(hops[0])
        z[2] = (z[0].astype(F32) + z[1].astype(F32)).astype(BF16)
        start(hops[1])

    t_hops = doubling(0, zt.at[0], zt.at[1], zt.at[2], zt.at[3])
    s_hops = doubling(4, zs.at[0], zs.at[1], zs.at[2], zs.at[3])
    e_hops = doubling(8, exact, exact_in1, exact_mid, exact_in2)
    rounded_start(t_hops, zt, top)

    keep_a = ((zz + 1) // 2) % 2
    keep_b = zz // 2
    last = zz % 2

    def cols_at(start_at, size):
        return pl.ds(pl.multiple_of(start_at, quarter), size)

    own_a, give_a = cols_at(keep_a * two, two), cols_at((1 - keep_a) * two, two)
    own_b = cols_at(2 * two + keep_b * two, two)
    give_b = cols_at(2 * two + (1 - keep_b) * two, two)
    q_own_a = cols_at(keep_a * two + last * quarter, quarter)
    q_give_a = cols_at(keep_a * two + (1 - last) * quarter, quarter)
    q_own_b = cols_at(2 * two + keep_b * two + last * quarter, quarter)
    q_give_b = cols_at(2 * two + keep_b * two + (1 - last) * quarter, quarter)
    full = v3.at[pl.ds(TRAITS, ROWS - TRAITS)]
    p_hops = (
        (
            zcopy(zp_part.at[:, give_a], zp_a1, 12, pair),
            zcopy(zp_part.at[:, give_b], zp_b1, 13, cross),
        ),
        (
            zcopy(zp_part.at[:, q_give_a], zp_a2, 14, cross),
            zcopy(zp_part.at[:, q_give_b], zp_b2, 15, pair),
        ),
        (
            zcopy(full.at[:, q_own_a], full.at[:, q_own_a], 16, cross),
            zcopy(full.at[:, q_own_b], full.at[:, q_own_b], 17, pair),
        ),
        (
            zcopy(full.at[:, own_a], full.at[:, own_a], 18, pair),
            zcopy(full.at[:, own_b], full.at[:, own_b], 19, cross),
        ),
    )

    def add_into(target, cols, extra):
        total = zp_part[:, cols].astype(F32) + extra[...].astype(F32)
        target[:, cols] = total.astype(BF16)

    def probes_hop1():
        finish(p_hops[0])
        add_into(zp_part, own_a, zp_a1)
        add_into(zp_part, own_b, zp_b1)
        start(p_hops[1])

    def probes_hop2():
        finish(p_hops[1])
        add_into(full, q_own_a, zp_a2)
        add_into(full, q_own_b, zp_b2)
        start(p_hops[2])

    def probes_hop3():
        finish(p_hops[2])
        start(p_hops[3])

    arrived(P1ALL, p1_all)
    drained(P1ALL, p1_all)

    @pl.loop(0, people // LANES)
    def _(t):
        cols = pl.ds(pl.multiple_of(t * LANES, LANES), LANES)
        pp[:64, cols] = p1_all[2 * t]
        pp[64:, cols] = p1_all[2 * t + 1]

    acc_p[...] = jnp.zeros_like(acc_p)

    def back_probes(lo, hi):
        @pl.loop(lo, hi)
        def _(j):
            acc_p[...] += jnp.dot(
                pp[:, rows_of(j)], geno[rows_of(j), :], preferred_element_type=F32
            )

    mid = (chunks + 1) // 2
    back_probes(0, mid)

    rounded_middle(t_hops, zt)

    back_probes(mid, chunks)

    @pl.loop(0, steps)
    def _(i):
        zp_part[:, columns(i)] = acc_p[TRAITS:, columns(i)].astype(BF16)

    finish(t_hops[1])
    start(p_hops[0])

    def residual_step(i, total):
        cols = columns(i)
        value = scale_c * (zt[2, :, cols].astype(F32) + zt[3, :, cols].astype(F32))
        v2[:, cols] = value.astype(BF16)
        return total + value * value

    squares = lax.fori_loop(0, steps, residual_step, jnp.zeros((TRAITS, width), F32))
    n0_col[:TRAITS, :] = jnp.sum(squares, axis=1, keepdims=True)

    @pl.loop(0, chunks)
    def _(j):
        value = lax.dot_general(v2[...], geno[rows_of(j), :], NT, preferred_element_type=F32)
        put_traits(t2_out, value, j)
        scatter_chunk(T2, j, t2_out, t2_in)

    probes_hop1()
    t2_in[me] = t2_out[me]

    arrived(T2, t2_in)
    t2_mine[...] = jnp.sum(t2_in[...], axis=0).astype(BF16)
    gather_all(T2ALL, t2_mine, t2_all, t2_sem.at[me // owners])
    t2_all[me] = t2_mine[...]
    rounded = t2_mine[...].astype(F32)
    q1_col[trait_rows, :] = jnp.sum(rounded * rounded, axis=1, keepdims=True)
    drained(T2, t2_in)

    probes_hop2()

    back_traits(T2ALL, t2_all, t2_sem, low)
    rounded_start(s_hops, zs, low)

    probes_hop3()

    rounded_middle(s_hops, zs)

    finish(p_hops[3])

    finish(s_hops[1])
    start(e_hops[0])

    @pl.loop(0, steps)
    def _(i):
        cols = columns(i)
        v3[:TRAITS, cols] = (zs[2, :, cols].astype(F32) + zs[3, :, cols].astype(F32)).astype(BF16)

    @pl.loop(0, chunks)
    def _(j):
        value = lax.dot_general(v3[...], geno[rows_of(j), :], NT, preferred_element_type=F32)
        put_rows(u_out, value, j)
        scatter_chunk(U, j, u_out, u_in)

    u_in[me] = u_out[me]

    finish(e_hops[0])

    @pl.loop(0, steps)
    def _(i):
        exact_mid[:, columns(i)] = exact[:, columns(i)] + exact_in1[:, columns(i)]

    start(e_hops[1])

    arrived(U, u_in)
    u = summed(u_in)
    mine = p1_mine[...].astype(F32)
    pieces = jnp.concatenate([t2_all[2 * tile], t2_all[2 * tile + 1]], axis=0).astype(F32)
    mine = jnp.concatenate([jnp.where(half == 0, pieces, mine[:TRAITS]), mine[TRAITS:]], axis=0)
    m2_col[wide_rows, :] = jnp.sum(u * mine, axis=1, keepdims=True)
    m3_col[wide_rows, :] = jnp.sum(u * u, axis=1, keepdims=True)

    lane = iota((ROWS, LANES), 1)
    moments = jnp.where(lane == 0, n0_col[...] * (1.0 / zsize), 0.0)
    moments = jnp.where(lane == 1, q1_col[...], moments)
    moments = jnp.where(lane == 2, m2_col[...], moments)
    moments = jnp.where(lane == 3, m3_col[...], moments)
    mom_out[...] = jnp.transpose(moments)[:4]
    gather_all(MOM, mom_out, mom_in)
    mom_in[me] = mom_out[...]
    drained(U, u_in)

    finish(e_hops[1])

    @pl.loop(0, steps)
    def _(i):
        cols = columns(i)
        r0[:, cols] = scale_c * (exact_mid[:TRAITS, cols] + exact_in2[:TRAITS, cols])
        back[:, cols] = exact_mid[TRAITS:, cols] + exact_in2[TRAITS:, cols]

    arrived(MOM, mom_in)
    zmom_out[...] = jnp.sum(mom_in[...], axis=0)

    def zmom(d):
        q = (zz + d) % zsize
        return zcopy(zmom_out, zmom_in.at[d], 19 + d, q)

    for d in range(1, zsize):
        zmom(d).start()
    zmom_in[0] = zmom_out[...]
    drained(MOM, mom_in)
    for d in range(1, zsize):
        zmom(d).wait()
    totals = jnp.zeros((4, LANES), F32)
    for q in range(zsize):
        totals = totals + zmom_in[(zz + zsize - q) % zsize]

    n0, q1, m2, m3 = totals[0:1], totals[1:2], totals[2:3], totals[3:4]
    step1 = n0 / (scale_row * q1 + lam_row * n0)
    shrunk = 1.0 - step1 * lam_row
    gain = step1 * scale_row
    n1 = shrunk * shrunk * n0 - 2.0 * shrunk * gain * q1 + gain * gain * m2
    beta = n1 / n0
    mix = shrunk + beta
    p2 = mix * mix * q1 - 2.0 * mix * gain * m2 + gain * gain * m3
    step2 = n1 / (scale_row * p2 + lam_row * (n1 + beta * beta * n0))
    is_probe = iota((1, LANES), 1) >= TRAITS
    dot_row = jnp.where(is_probe, step1 * n0 + step2 * n1, 0.0)
    norm_row = jnp.where(is_probe, n0, 0.0)
    for shift in (16, 32, 64):
        dot_row = dot_row + pltpu.roll(dot_row, shift, 1)
        norm_row = norm_row + pltpu.roll(norm_row, shift, 1)
    eta = lam_row * dot_row / (norm_row + 1e-6)
    next_prec = lam_row * (1.0 - eta) / eta
    slab_var = slab_row / prec_row
    next_shrink = slab_var * next_prec / (1.0 + slab_var * next_prec)
    next_base = odds_row + 0.5 * jnp.log(1.0 - next_shrink)
    lane = iota((TRAITS, LANES), 1)
    table = jnp.zeros((TRAITS, LANES), F32)
    for k, row in enumerate(
        (step1 + step2 * mix, step2 * gain, eta, next_prec, next_shrink, next_base)
    ):
        table = jnp.where(lane == k, to_column(row), table)
    coefs[...] = table


def per_device(
    genotypes, phenotypes, message, probes, inclusion, slab_ratio, input_precision, noise_precision
):
    people, markers = genotypes.shape
    zsize, group = lax.axis_size("sample"), lax.axis_size("marker")
    assert group == 2 * people // LANES and zsize == 4
    assert message.shape[0] == TRAITS and probes.shape[0] == ROWS - TRAITS
    chunks = max(1, people // 512)
    rest = ROWS - TRAITS
    quarter = markers // 8
    vmem = pltpu.VMEM
    dma = pltpu.SemaphoreType.DMA
    whole = pl.BlockSpec(memory_space=pltpu.VMEM)
    far = pl.BlockSpec(memory_space=pl.ANY)
    scalars = pl.BlockSpec(memory_space=pltpu.SMEM)
    out = jax.ShapeDtypeStruct((TRAITS, markers), F32)
    piece_t = vmem((group, 8, LANES), F32)
    piece_b = vmem((group, 8, LANES), BF16)
    piece_p = vmem((group, 64, LANES), BF16)
    trait_all = vmem((TRAITS, markers), F32)
    exact = vmem((2 * TRAITS, markers), F32)
    column = vmem((ROWS, 1), F32)
    centre, r0, back, coefs = pl.pallas_call(
        functools.partial(kernel, float(people * zsize), float(markers * group)),
        out_shape=(out, out, out, jax.ShapeDtypeStruct((TRAITS, LANES), F32)),
        in_specs=[far, far, far, far, scalars, scalars, scalars, scalars],
        out_specs=(whole, whole, whole, whole),
        scratch_shapes=[
            vmem((people, markers), BF16),
            vmem((TRAITS, people), F32),
            trait_all,
            vmem((rest, markers), F32),
            vmem((4 * TRAITS + rest, markers), BF16),
            vmem((TRAITS, markers), BF16),
            vmem((ROWS, markers), BF16),
            vmem((1, LANES), F32),
            vmem((group, 1, LANES), F32),
            vmem((4 * TRAITS, people), F32),
            piece_t,
            piece_t,
            vmem((8, LANES), BF16),
            piece_b,
            piece_p,
            piece_p,
            vmem((64, LANES), BF16),
            piece_p,
            piece_t,
            piece_t,
            vmem((8, LANES), BF16),
            piece_b,
            piece_p,
            piece_p,
            vmem((TRAITS, people), BF16),
            vmem((ROWS, people), BF16),
            vmem((ROWS, markers), F32),
            exact,
            exact,
            exact,
            exact,
            vmem((4, TRAITS, markers), BF16),
            vmem((4, TRAITS, markers), BF16),
            vmem((rest, markers), BF16),
            vmem((rest, 2 * quarter), BF16),
            vmem((rest, 2 * quarter), BF16),
            vmem((rest, quarter), BF16),
            vmem((rest, quarter), BF16),
            column,
            column,
            column,
            column,
            vmem((4, LANES), F32),
            vmem((group, 4, LANES), F32),
            vmem((4, LANES), F32),
            vmem((zsize, 4, LANES), F32),
            dma((chunks,)),
            dma((3,)),
            dma((9,)),
            dma((9,)),
            dma((chunks,)),
            dma((chunks,)),
            dma((20 + zsize,)),
            dma((20 + zsize,)),
        ],
        compiler_params=pltpu.CompilerParams(
            collective_id=0, has_side_effects=True, vmem_limit_bytes=56 << 20
        ),
        name="vamp_round",
    )(
        genotypes,
        phenotypes,
        message,
        probes,
        inclusion,
        slab_ratio,
        input_precision,
        noise_precision,
    )
    along_r, along_b, eta, prec, shrink, base = (coefs[:, k : k + 1] for k in range(6))
    lmmse = centre + along_r * r0 - along_b * back
    signal = (lmmse - eta * centre) / (1.0 - eta)
    return denoise(signal, prec, shrink, base)[0], lmmse


def solution(mesh):
    return jax.shard_map(
        per_device,
        mesh=mesh,
        in_specs=(
            P("sample", "marker"),
            P(None, "sample"),
            P(None, "marker"),
            P(None, "marker"),
            P(),
            P(),
            P(),
            P(),
        ),
        out_specs=(P(None, "marker"), P(None, "marker")),
        check_vma=False,
    )
```

time: 121 us -> 94.1 us (0.78)
  Pallas kernels: 117 us -> 89.9 us
  local copies, waits for them, and re-layouts: 3.34 us -> 0 us
  other arithmetic: 0 us -> 3.33 us
    pallas_call x1, Pallas kernels: 117 us -> 89.9 us  [per_device(): pl.pallas_call(functools.partial(kernel, float(people * zsize), float(mar...]
    unnamed x2 -> x0, local copies, waits for them, and re-layouts: 3.34 us -> none
    mul x0 -> x1, other arithmetic: none -> 2.11 us  [denoise(): shrink * weight * signal]
    slice x0 -> x1, other arithmetic: none -> 1.21 us  [per_device(): coefs[:, k:k + 1]]
where the time goes in v2:
time: 94.1 us; the launch traced here: 93.9 us
  Pallas kernels  89.9 us (96%)
  other arithmetic  3.33 us (4%)
    pallas_call x1, Pallas kernels, per_device(): pl.pallas_call(functools.partial(kernel, float(people * zsize), float(mar...  89.9 us
    mul x1, other arithmetic, denoise(): shrink * weight * signal  2.11 us

profile of v2, /device:TPU:1, one launch (start us, length us, event | category | flops | bytes accessed | tf_op | source)
XLA Modules:
  0.0 93.9 jit_solution(3295896455758253017)
XLA Ops:
  0.6 89.9 %vamp_round.1 = (f32[16,4096]{1,0:T(8,128)}, f32[16,4096]{1,0:T(8,128)}, f32[16,4096]{1,0:T(8,128)}, f32[16,128]{1,0:T(8,128)}) custom-call(bf16[2048,4096]{1,0:T(8,128)(2,1)} %geno_hbm.1, f32[16,2048]{1,0:T(8,128)} %pheno_hbm.1, f32[16,4096]{1,0:T(8,128)} %message_hbm.1, f32[112,4096]{1,0:T(8,128)} %probes_hbm.1, f32[16]{0:T(128)} %incl.1, f32[16]{0:T(128)} %slab.1, ...), custom_call_target="tpu_custom_call" | custom-call | tf_op jit(solution)/shard_map/vamp_round/pallas_call | solution.py:655
  90.5 1.2 %slice_reduce_fusion.4 = (f32[16]{0:T(128)S(1)}, f32[16]{0:T(128)S(1)}, f32[16]{0:T(128)S(1)}, f32[16]{0:T(128)S(1)}, f32[16]{0:T(128)S(1)}, /*index=5*/f32[16]{0:T(128)S(1)}, f32[16]{0:T(128)S(1)}) fusion(f32[16,128]{1,0:T(8,128)} %get-tuple-element.6), kind=kLoop, calls=%fused_computation.16 | loop fusion | flops 32 | bytes 832 | tf_op jit(solution)/shard_map/slice | solution.py:730
  91.8 2.1 %fusion.7 = (f32[16,4096]{1,0:T(8,128)}, f32[16,4096]{1,0:T(8,128)}) fusion(f32[16,4096]{1,0:T(8,128)} %get-tuple-element.7, f32[16]{0:T(128)S(1)} %get-tuple-element.11, f32[16]{0:T(128)S(1)} %get-tuple-element.12, f32[16]{0:T(128)S(1)} %get-tuple-element.15, f32[16]{0:T(128)S(1)} %get-tuple-element.16, f32[16]{0:T(128)S(1)} %get-tuple-element.10, ...), kind=kLoop, calls=%fused_computation.8 | loop fusion | flops 1048576 | bytes 1311168 | tf_op jit(solution)/shard_map/mul | solution.py:22
